TPU v7x, 32 devices: a whole 2x2x4 slice. The times are simulated.
32 devices in a mesh: fsdp: 4 (over z), ctx: 4 (over x, core), tp: 2 (over y).
Axes of the slice: x: 2, y: 2, z: 4, core: 2. Of those that a mesh axis runs over, the one named last changes fastest.
Arguments:
- tokens: bfloat16 [4, 1536, 2048], P('fsdp', 'ctx'), may hold values from -6 to 6
- seq_ids: int32 [4, 1536], P('fsdp'), may hold values from 0 to 2, never falling along the last dimension, each value on 1 to 768 neighbouring positions
- pic_starts: int32 [4, 3], P('fsdp'), may hold values from 0 to 1408, as said below
- pic_lengths: int32 [4, 3], P('fsdp'), may hold values from 128 to 256, as said below
- skip_mask: int32 [4, 1536], P('fsdp', 'ctx'), may hold values 0 or 1
- w_query: bfloat16 [2048, 2048], P('fsdp', 'tp'), may hold values from -0.125 to 0.125
- w_key: bfloat16 [2048, 512], P('fsdp', 'tp'), may hold values from -0.125 to 0.125
- w_value: bfloat16 [2048, 512], P('fsdp', 'tp'), may hold values from -0.125 to 0.125
- w_out: bfloat16 [2048, 2048], P('tp', 'fsdp'), may hold values from -1 to 1
- w_gate: bfloat16 [2048, 5632], P('fsdp', 'tp'), may hold values from -0.125 to 0.125
- w_up: bfloat16 [2048, 5632], P('fsdp', 'tp'), may hold values from -0.125 to 0.125
- w_down: bfloat16 [5632, 2048], P('tp', 'fsdp'), may hold values from -0.078125 to 0.078125
- gain_attn: bfloat16 [2048], P('fsdp'), may hold values from 0.25 to 1.75
- gain_ffn: bfloat16 [2048], P('fsdp'), may hold values from 0.25 to 1.75
- cotangent: bfloat16 [4, 1536, 2048], P('fsdp', 'ctx'), may hold values from -6 to 6
Outputs:
- output: bfloat16 [4, 1536, 2048], P('fsdp', 'ctx')
- input_grad: bfloat16 [4, 1536, 2048], P('fsdp', 'ctx')
- grad_query: float32 [2048, 2048], P('fsdp', 'tp')
- grad_key: float32 [2048, 512], P('fsdp', 'tp')
- grad_value: float32 [2048, 512], P('fsdp', 'tp')
- grad_out: float32 [2048, 2048], P('tp', 'fsdp')
- grad_gate: float32 [2048, 5632], P('fsdp', 'tp')
- grad_up: float32 [2048, 5632], P('fsdp', 'tp')
- grad_down: float32 [5632, 2048], P('tp', 'fsdp')
- grad_gain_attn: float32 [2048], P('fsdp')
- grad_gain_ffn: float32 [2048], P('fsdp')
Inputs may be any that keep to these rules, and one draw needn't show every extreme that they name: `pic_starts`: picture p of a row (counting from 0) lies inside positions p * 2 * 256 to (p + 1) * 2 * 256 - 1, so pictures never intersect; it may start anywhere in that range where it fits. `pic_lengths`: every row has a picture of exactly 256 positions and another of exactly 128.
All inputs are finite; a program needn't handle non-finite values. No bound on the sum of `skip_mask` on one device may be relied on, other than what follows from the above.
Results may differ from a plain program's by a relative error of at most 0.022.
Values may be sent and summed in bfloat16 or wider, within the bound.
No kernel may reach another device: no remote copies, remote signals or barrier semaphores. Data moves between devices by JAX's collectives and lax.ppermute only.
A program may use at most 256 MiB of HBM per device.

v0:
```python
import math
import jax
import jax.numpy as jnp
from jax import lax
from jax.sharding import PartitionSpec as P

HEAD = 128
norm_eps = 1e-05
rope_base = 10000.0
F32 = jnp.float32
BF16 = jnp.bfloat16


def dot(a, b, ca, cb):
    return lax.dot_general(a, b, (((ca,), (cb,)), ((), ())), preferred_element_type=F32)


def rope_tables(positions):
    half_width = HEAD // 2
    frequency = jnp.power(rope_base, -jnp.arange(half_width, dtype=F32) * 2.0 / HEAD)
    angles = positions.astype(F32)[:, None] * frequency[None, :]
    return (jnp.cos(angles), jnp.sin(angles))


def rotate(u, cosine, sine):
    half_width = HEAD // 2
    parts = []
    for head in range(u.shape[1] // HEAD):
        first = u[:, head * HEAD : head * HEAD + half_width]
        second = u[:, head * HEAD + half_width : (head + 1) * HEAD]
        parts += [first * cosine - second * sine, second * cosine + first * sine]
    return jnp.concatenate(parts, axis=1)


def picture_ids(starts, lengths, positions):
    inside = (positions[:, None] >= starts[None, :]) & (
        positions[:, None] < starts[None, :] + lengths[None, :]
    )
    numbers = jnp.arange(1, starts.shape[0] + 1, dtype=jnp.int32)
    return jnp.sum(jnp.where(inside, numbers[None, :], 0), axis=1)


def allowed_mask(query_pos, key_pos, query_doc, key_doc, query_pic, key_pic):
    same_doc = query_doc[:, None] == key_doc[None, :]
    causal = key_pos[None, :] <= query_pos[:, None]
    picture = (query_pic[:, None] == key_pic[None, :]) & (query_pic[:, None] > 0)
    return same_doc & (causal | picture)


def norm_back(d_normed, hat, inv_rms, gain):
    scaled = d_normed * gain
    return inv_rms * (scaled - hat * jnp.mean(scaled * hat, axis=-1, keepdims=True))


def far(v):
    return lax.ppermute(v, "ctx", [(i, i ^ 2) for i in range(4)])


def near(v):
    return lax.ppermute(v, "ctx", [(i, i ^ 1) for i in range(4)])


def side(v):
    return lax.ppermute(v, "tp", [(0, 1), (1, 0)])


def spread(v):
    n, w = v.shape
    left, right = (v[:, : w // 2], v[:, w // 2 :])
    left_far = far(left)
    right_side = side(right)
    left_two = side(jnp.concatenate([left, left_far], axis=0))
    right_two = far(jnp.concatenate([right, right_side], axis=0))
    left_all = jnp.concatenate([left, left_two[:n], left_far, left_two[n:]], axis=0)
    right_all = jnp.concatenate([right, right_side, right_two], axis=0)
    mine = jnp.concatenate([left_all, right_all], axis=1)
    return jnp.concatenate([mine, near(mine)], axis=0)


def collect(p):
    n, w = (p.shape[0] // 8, p.shape[1])
    both = p[: 4 * n].astype(F32) + near(p[4 * n :]).astype(F32)
    both = both.astype(BF16)
    left, right = (both[:, : w // 2], both[:, w // 2 :].reshape(2, 2, n, w // 2))
    left_far = far(left[2 * n :])
    right_side = side(right[:, 1].reshape(2 * n, w // 2))
    left = (left[: 2 * n].astype(F32) + left_far.astype(F32)).astype(BF16)
    right = (right[:, 0].reshape(2 * n, w // 2).astype(F32) + right_side.astype(F32)).astype(BF16)
    left_side = side(left[n:])
    right_far = far(right[n:])
    return jnp.concatenate(
        [
            left[:n].astype(F32) + left_side.astype(F32),
            right[:n].astype(F32) + right_far.astype(F32),
        ],
        axis=1,
    )


def both_sides(v, t):
    other = side(v)
    return jnp.where(
        t == 0, jnp.concatenate([v, other], axis=0), jnp.concatenate([other, v], axis=0)
    )


def ctx_rows(v, c):
    n = v.shape[0]
    two = jnp.stack([v, far(v)])
    other = near(two)
    out = jnp.zeros((4, n, v.shape[1]), v.dtype)
    for bits, piece in ((0, two[0]), (2, two[1]), (1, other[0]), (3, other[1])):
        out = lax.dynamic_update_slice(out, piece[None], (c ^ bits, 0, 0))
    return out


def swap_halves(v):
    n = v.shape[0] // 2
    return jnp.concatenate([v[n:], v[:n]], axis=0)


def body(
    tokens,
    seq_ids,
    pic_starts,
    pic_lengths,
    skip_mask,
    w_query,
    w_key,
    w_value,
    w_out,
    w_gate,
    w_up,
    w_down,
    gain_attn,
    gain_ffn,
    cotangent,
):
    tok_rows = tokens.shape[1]
    width = tokens.shape[2]
    own = tok_rows // 2
    seq_len = seq_ids.shape[1]
    c = lax.axis_index("ctx")
    t = lax.axis_index("tp")
    core = c & 1
    q_cols = w_query.shape[1] // 4
    heads = q_cols // HEAD
    ff = w_gate.shape[1] // 4
    query_scale = 1.0 / math.sqrt(HEAD)
    wq_t = lax.dynamic_slice_in_dim(w_query, c * q_cols, q_cols, 1).T
    w_kv = jnp.where(core == 0, w_key, w_value)
    wkv_t = lax.dynamic_slice_in_dim(w_kv, (c >> 1) * HEAD, HEAD, 1).T
    gains = jnp.concatenate(
        [gain_attn[None], gain_ffn[None], jnp.zeros((14, gain_attn.shape[0]), BF16)], axis=0
    )
    first = lax.all_gather(
        jnp.concatenate([wq_t, wkv_t, gains], axis=0), "fsdp", axis=1, tiled=True
    )
    qkv_cols = q_cols + HEAD
    wqkv = first[:qkv_cols]
    gain_one = first[qkv_cols].astype(F32)
    gain_two = first[qkv_cols + 1].astype(F32)
    wo = lax.all_gather(
        lax.dynamic_slice_in_dim(w_out, c * q_cols, q_cols, 0), "fsdp", axis=1, tiled=True
    )
    wg_t = lax.dynamic_slice_in_dim(w_gate, c * ff, ff, 1).T
    wu_t = lax.dynamic_slice_in_dim(w_up, c * ff, ff, 1).T
    wgu = lax.all_gather(jnp.concatenate([wg_t, wu_t], axis=0), "fsdp", axis=1, tiled=True)
    wd = lax.all_gather(lax.dynamic_slice_in_dim(w_down, c * ff, ff, 0), "fsdp", axis=1, tiled=True)
    x_own_b = lax.dynamic_slice_in_dim(tokens[0], t * own, own, 0)
    x_own = x_own_b.astype(F32)
    keep_own = lax.dynamic_slice_in_dim(skip_mask[0], t * own, own, 0).astype(F32)[:, None]
    dy_own = lax.dynamic_slice_in_dim(cotangent[0], t * own, own, 0).astype(F32)
    d_ffn_own = (keep_own * dy_own).astype(BF16)
    pos_list = []
    for block in range(8):
        near_bit, far_bit, side_bit = (block >> 2, block >> 1 & 1, block & 1)
        start = (c ^ near_bit + 2 * far_bit) * tok_rows + (t ^ side_bit) * own
        pos_list.append(start)
    positions = jnp.concatenate([s + jnp.arange(own, dtype=jnp.int32) for s in pos_list])
    docs = jnp.concatenate([lax.dynamic_slice_in_dim(seq_ids[0], s, own, 0) for s in pos_list])
    pics = picture_ids(pic_starts[0], pic_lengths[0], positions)
    allowed = allowed_mask(positions, positions, docs, docs, pics, pics)
    cosine, sine = rope_tables(positions)
    x_all = spread(x_own_b).astype(F32)
    inv_all = lax.rsqrt(jnp.mean(x_all * x_all, axis=-1, keepdims=True) + norm_eps)
    n1 = (x_all * inv_all * gain_one).astype(BF16)
    qkv_pre = dot(n1, wqkv, 1, 1)
    queries = (rotate(qkv_pre[:, :q_cols], cosine, sine) * query_scale).astype(BF16)
    kv_pre = qkv_pre[:, q_cols:]
    kv_own = jnp.where(core == 0, rotate(kv_pre, cosine, sine), kv_pre).astype(BF16)
    kv_other = swap_halves(near(kv_own))
    keys = jnp.where(core == 0, kv_own, kv_other)
    values = jnp.where(core == 0, kv_other, kv_own)
    q_heads = queries.reshape(seq_len, heads, HEAD)
    scores = jnp.einsum("qhd,kd->hqk", q_heads, keys, preferred_element_type=F32)
    masked = jnp.where(allowed[None], scores, -1e30)
    row_max = jnp.max(masked, axis=-1, keepdims=True)
    exp_scores = jnp.exp(masked - row_max)
    row_total = jnp.sum(exp_scores, axis=-1, keepdims=True)
    soft_b = (exp_scores / row_total).astype(BF16)
    log_total = row_max + jnp.log(row_total)
    head_out = (
        jnp.einsum("hqk,kd->qhd", soft_b, values, preferred_element_type=F32)
        .reshape(seq_len, q_cols)
        .astype(BF16)
    )
    attn = collect(dot(head_out, wo, 1, 0).astype(BF16))
    mid = x_own + keep_own * attn
    inv_two = lax.rsqrt(jnp.mean(mid * mid, axis=-1, keepdims=True) + norm_eps)
    hat_two = mid * inv_two
    n2 = spread((hat_two * gain_two).astype(BF16))
    d_ffn = spread(d_ffn_own)
    gu = dot(wgu, n2, 1, 1)
    gate, up = (gu[:ff], gu[ff:])
    sig = jax.nn.sigmoid(gate)
    hidden = (gate * sig * up).astype(BF16)
    d_hidden = dot(wd, d_ffn, 1, 1)
    d_gate = (d_hidden * up * sig * (1.0 + gate * (1.0 - sig))).astype(BF16)
    d_up = (d_hidden * (gate * sig)).astype(BF16)
    d_gu = jnp.concatenate([d_gate, d_up], axis=0)
    d_n2 = collect(dot(d_gu, wgu, 0, 0).astype(BF16))
    grad_gu = dot(d_gu, n2, 1, 0).astype(BF16)
    grad_down = dot(hidden, d_ffn, 1, 0).astype(BF16)
    shard_gu = lax.psum_scatter(grad_gu, "fsdp", scatter_dimension=1, tiled=True)
    shard_down = lax.psum_scatter(grad_down, "fsdp", scatter_dimension=1, tiled=True)
    ffn = collect(dot(hidden, wd, 0, 0).astype(BF16))
    output = both_sides((mid + keep_own * ffn).astype(BF16), t)
    d_mid = dy_own + norm_back(d_n2, hat_two, inv_two, gain_two)
    d_attn = spread((keep_own * d_mid).astype(BF16))
    grad_out = dot(head_out, d_attn, 0, 0).astype(BF16)
    shard_out = lax.psum_scatter(grad_out, "fsdp", scatter_dimension=1, tiled=True)
    d_head = dot(d_attn, wo, 1, 1).astype(BF16).reshape(seq_len, heads, HEAD)
    scores = jnp.einsum("qhd,kd->hqk", q_heads, keys, preferred_element_type=F32)
    soft = jnp.where(allowed[None], jnp.exp(scores - log_total), 0.0)
    d_soft = jnp.einsum("qhd,kd->hqk", d_head, values, preferred_element_type=F32)
    delta = jnp.sum(soft * d_soft, axis=-1, keepdims=True)
    d_scores = (soft * (d_soft - delta)).astype(BF16)
    d_queries = jnp.einsum("hqk,kd->qhd", d_scores, keys, preferred_element_type=F32)
    d_keys = jnp.einsum("hqk,qhd->kd", d_scores, q_heads, preferred_element_type=F32)
    d_values = jnp.einsum("hqk,qhd->kd", soft.astype(BF16), d_head, preferred_element_type=F32)
    sent = swap_halves(near(jnp.where(core == 0, d_values, d_keys).astype(BF16)))
    d_kv = jnp.where(core == 0, d_keys, d_values) + sent.astype(F32)
    d_kv_pre = jnp.where(core == 0, rotate(d_kv, cosine, -sine), d_kv)
    d_query_pre = rotate(d_queries.reshape(seq_len, q_cols), cosine, -sine) * query_scale
    d_qkv = jnp.concatenate([d_query_pre.astype(BF16), d_kv_pre.astype(BF16)], axis=1)
    grad_qkv = dot(d_qkv, n1, 0, 0).astype(BF16)
    shard_qkv = lax.psum_scatter(grad_qkv, "fsdp", scatter_dimension=1, tiled=True)
    d_n1 = collect(dot(d_qkv, wqkv, 1, 0).astype(BF16))
    inv_one = lax.rsqrt(jnp.mean(x_own * x_own, axis=-1, keepdims=True) + norm_eps)
    hat_one = x_own * inv_one
    input_grad = both_sides((d_mid + norm_back(d_n1, hat_one, inv_one, gain_one)).astype(BF16), t)
    gain_grads = lax.psum(
        jnp.stack([jnp.sum(d_n1 * hat_one, axis=0), jnp.sum(d_n2 * hat_two, axis=0)]),
        ("fsdp", "ctx", "tp"),
    )
    shard_width = gain_attn.shape[0]
    gain_grads = lax.dynamic_slice_in_dim(
        gain_grads, lax.axis_index("fsdp") * shard_width, shard_width, 1
    )
    all_gu = ctx_rows(shard_gu, c)
    all_down = ctx_rows(shard_down, c).reshape(4 * ff, -1)
    all_out = ctx_rows(shard_out, c).reshape(4 * q_cols, -1)
    all_qkv = ctx_rows(shard_qkv, c)
    grad_kv = all_qkv[:, q_cols:].reshape(2, 2, HEAD, -1)
    return (
        output[None],
        input_grad[None],
        all_qkv[:, :q_cols].reshape(4 * q_cols, -1).T.astype(F32),
        grad_kv[:, 0].reshape(2 * HEAD, -1).T.astype(F32),
        grad_kv[:, 1].reshape(2 * HEAD, -1).T.astype(F32),
        all_out.astype(F32),
        all_gu[:, :ff].reshape(4 * ff, -1).T.astype(F32),
        all_gu[:, ff:].reshape(4 * ff, -1).T.astype(F32),
        all_down.astype(F32),
        gain_grads[0],
        gain_grads[1],
    )


def solution(mesh):
    placed = (
        P("fsdp", "ctx", None),
        P("fsdp", None),
        P("fsdp", None),
        P("fsdp", None),
        P("fsdp", "ctx"),
        P("fsdp", "tp"),
        P("fsdp", "tp"),
        P("fsdp", "tp"),
        P("tp", "fsdp"),
        P("fsdp", "tp"),
        P("fsdp", "tp"),
        P("tp", "fsdp"),
        P("fsdp"),
        P("fsdp"),
        P("fsdp", "ctx", None),
    )
    return jax.shard_map(
        body,
        mesh=mesh,
        in_specs=placed,
        out_specs=(
            P("fsdp", "ctx", None),
            P("fsdp", "ctx", None),
            P("fsdp", "tp"),
            P("fsdp", "tp"),
            P("fsdp", "tp"),
            P("tp", "fsdp"),
            P("fsdp", "tp"),
            P("fsdp", "tp"),
            P("tp", "fsdp"),
            P("fsdp"),
            P("fsdp"),
        ),
        check_vma=False,
    )
```

profile of v0, /device:TPU:0, one launch (start us, length us, event | category | flops | bytes accessed | tf_op | source)
XLA Modules:
  0.0 825.5 jit_solution(8399771713944028795)
XLA Ops:
  20.2 7.6 collective-permute-done
  31.3 15.3 %collective-permute-done.1 = bf16[384,1024]{1,0:T(8,128)(2,1)S(1)} collective-permute-done((bf16[384,1024]{1,0:T(8,128)(2,1)S(1)}, bf16[384,1024]{1,0:T(8,128)(2,1)S(1)}, u32[]{:S(2)}, u32[]{:S(2)}) %collective-permute-start.1) | collective-permute-done | bytes 786464 | tf_op jit(solution)/shard_map/ppermute | solution.py:64
  47.9 19.6 %maximum_maximum_fusion = bf16[768,2048]{1,0:T(8,128)(2,1)} fusion(bf16[384,1024]{1,0:T(8,128)(2,1)S(1)} %collective-permute-done.3, bf16[192,1024]{1,0:T(8,128)(2,1)S(1)} %collective-permute-done.2, bf16[192,1024]{1,0:T(8,128)(2,1)S(1)} %get-tuple-element.104, bf16[192,1024]{1,0:T(8,128)(2,1)S(1)} %get-tuple-element.102, ...), kind=kLoop, calls=%fused_computation.45 | loop fusion | flops 22020096 | bytes 6291456 | tf_op jit(solution)/shard_map/concatenate | solution.py:76
  103.3 8.3 %fusion.16 = bf16[128,2,1536]{2,0,1:T(8,128)(2,1)} fusion(f32[1536,1536,2]{1,0,2:T(8,128)S(1)} %get-tuple-element.123, f32[2,1536]{1,0:T(2,128)S(1)} %fusion.6, f32[2,1536]{1,0:T(2,128)S(1)} %get-tuple-element.122, pred[1536,1536]{0,1:T(8,128)(4,1)} %or_and_fusion, bf16[1536,128]{0,1:T(8,128)(2,1)S(1)} %fusion.55, pred[]{:T(512)S(6)} %eq.48, ...), kind=kOutput, calls=%fused_computation.54 | convolution fusion | flops 1228210176 | bytes 22831104 | tf_op jit(solution)/shard_map/hqk,kd->qhd/dot_general | solution.py:204
  132.2 17.4 %collective-permute-done.7 = bf16[384,1024]{1,0:T(8,128)(2,1)S(1)} collective-permute-done((bf16[384,1024]{1,0:T(8,128)(2,1)S(1)}, bf16[384,1024]{1,0:T(8,128)(2,1)S(1)}, u32[]{:S(2)}, u32[]{:S(2)}) %collective-permute-start.7) | collective-permute-done | bytes 786464 | tf_op jit(solution)/shard_map/ppermute | solution.py:56
  152.6 7.9 collective-permute-done.8
  165.9 6.9 collective-permute-done.22
  178.1 15.3 %collective-permute-done.23 = bf16[384,1024]{1,0:T(8,128)(2,1)S(1)} collective-permute-done((bf16[384,1024]{1,0:T(8,128)(2,1)S(1)}, bf16[384,1024]{1,0:T(8,128)(2,1)S(1)}, u32[]{:S(2)}, u32[]{:S(2)}) %collective-permute-start.23) | collective-permute-done | bytes 786464 | tf_op jit(solution)/shard_map/ppermute | solution.py:64
  195.3 19.8 %maximum_maximum_fusion.2 = bf16[768,2048]{1,0:T(8,128)(2,1)} fusion(bf16[384,1024]{1,0:T(8,128)(2,1)S(1)} %collective-permute-done.25, bf16[192,1024]{1,0:T(8,128)(2,1)S(1)} %collective-permute-done.24, bf16[192,1024]{1,0:T(8,128)(2,1)S(1)} %get-tuple-element.96, bf16[192,1024]{1,0:T(8,128)(2,1)S(1)} %get-tuple-element.94, ...), kind=kLoop, calls=%fused_computation.47 | loop fusion | flops 22020096 | bytes 6291456 | tf_op jit(solution)/shard_map/concatenate | solution.py:76
  217.2 18.0 %collective-permute-done.12 = bf16[384,1024]{1,0:T(8,128)(2,1)S(1)} collective-permute-done((bf16[384,1024]{1,0:T(8,128)(2,1)S(1)}, bf16[384,1024]{1,0:T(8,128)(2,1)S(1)}, u32[]{:S(2)}, u32[]{:S(2)}) %collective-permute-start.12) | collective-permute-done | bytes 786464 | tf_op jit(solution)/shard_map/ppermute | solution.py:64
  235.8 20.0 %maximum_maximum_fusion.1 = bf16[768,2048]{1,0:T(8,128)(2,1)} fusion(bf16[384,1024]{1,0:T(8,128)(2,1)S(1)} %collective-permute-done.14, bf16[192,1024]{1,0:T(8,128)(2,1)S(1)} %collective-permute-done.13, bf16[192,1024]{1,0:T(8,128)(2,1)S(1)} %get-tuple-element.100, bf16[192,1024]{1,0:T(8,128)(2,1)S(1)} %get-tuple-element.98, ...), kind=kLoop, calls=%fused_computation.46 | loop fusion | flops 22020096 | bytes 6291456 | tf_op jit(solution)/shard_map/concatenate | solution.py:76
  256.9 7.3 pad_maximum_fusion.2
  264.3 35.1 %fusion.121 = f32[1408,1536]{1,0:T(8,128)} fusion(bf16[1408,2048]{0,1:T(8,128)(2,1)} %all-gather.9.cloned.1.call-done, bf16[768,2048]{1,0:T(8,128)(2,1)} %collective-permute-done.15, bf16[384,1024]{1,0:T(8,128)(2,1)} %copy-done.73, bf16[192,1024]{1,0:T(8,128)(2,1)S(1)} %copy-done.61, bf16[192,1024]{1,0:T(8,128)(2,1)S(1)} %copy-done.42, ...), kind=kOutput, calls=%fused_computation.277 | convolution fusion | flops 8908701696 | bytes 20709376 | tf_op jit(solution)/shard_map/dot_general | solution.py:15
  299.4 17.1 %all-gather.11.cloned.1.call-done = bf16[704,2048]{1,0:T(8,128)(2,1)} async-done(((bf16[704,512]{1,0:T(8,128)(2,1)}), bf16[704,2048]{1,0:T(8,128)(2,1)}) %all-gather.11.cloned.1.call-update) | async-done | bytes 2883600 | tf_op jit(solution)/shard_map/all_gather | solution.py:169
  316.5 13.8 %multiply_convert_fusion.1 = (bf16[704,1536]{1,0:T(8,128)(2,1)S(1)}, bf16[704,1536]{1,0:T(8,128)(2,1)}, bf16[704,1536]{1,0:T(8,128)(2,1)S(1)}) fusion(f32[1408,1536]{1,0:T(8,128)} %fusion.121, bf16[704,2048]{1,0:T(8,128)(2,1)} %all-gather.11.cloned.1.call-done, bf16[1536,2048]{1,0:T(8,128)(2,1)} %pad_maximum_fusion.2), kind=kOutput, calls=%fused_computation.40 | convolution fusion | flops 4445405184 | bytes 24313856 | tf_op jit(solution)/shard_map/dot_general | solution.py:15
  330.3 12.3 %convolution_convert_fusion.3 = bf16[1536,2048]{1,0:T(8,128)(2,1)S(1)} fusion(bf16[1408,2048]{0,1:T(8,128)(2,1)S(1)} %copy-done.93, bf16[704,1536]{1,0:T(8,128)(2,1)} %get-tuple-element.48, bf16[704,1536]{1,0:T(8,128)(2,1)S(1)} %get-tuple-element.47), kind=kOutput, calls=%fused_computation.26 | convolution fusion | flops 8870166528 | bytes 16384000 | tf_op jit(solution)/shard_map/dot_general | solution.py:15
  356.6 6.4 convolution_convert_fusion.5
  376.5 11.5 %collective-permute-done.28 = bf16[384,1024]{1,0:T(8,128)(2,1)S(1)} collective-permute-done((bf16[384,1024]{1,0:T(8,128)(2,1)S(1)}, bf16[384,1024]{1,0:T(8,128)(2,1)S(1)}, u32[]{:S(2)}, u32[]{:S(2)}) %collective-permute-start.28) | collective-permute-done | bytes 786464 | tf_op jit(solution)/shard_map/ppermute | solution.py:56
  391.8 13.0 %collective-permute-done.17 = bf16[384,1024]{1,0:T(8,128)(2,1)S(1)} collective-permute-done((bf16[384,1024]{1,0:T(8,128)(2,1)S(1)}, bf16[384,1024]{1,0:T(8,128)(2,1)S(1)}, u32[]{:S(2)}, u32[]{:S(2)}) %collective-permute-start.17) | collective-permute-done | bytes 786464 | tf_op jit(solution)/shard_map/ppermute | solution.py:56
  428.4 7.9 collective-permute-done.32
  438.6 15.2 %collective-permute-done.33 = bf16[384,1024]{1,0:T(8,128)(2,1)S(1)} collective-permute-done((bf16[384,1024]{1,0:T(8,128)(2,1)S(1)}, bf16[384,1024]{1,0:T(8,128)(2,1)S(1)}, u32[]{:S(2)}, u32[]{:S(2)}) %collective-permute-start.33) | collective-permute-done | bytes 786464 | tf_op jit(solution)/shard_map/ppermute | solution.py:64
  455.1 19.7 %maximum_maximum_fusion.3 = bf16[768,2048]{1,0:T(8,128)(2,1)} fusion(bf16[384,1024]{1,0:T(8,128)(2,1)S(1)} %collective-permute-done.35, bf16[192,1024]{1,0:T(8,128)(2,1)S(1)} %collective-permute-done.34, bf16[192,1024]{1,0:T(8,128)(2,1)S(1)} %get-tuple-element.92, bf16[192,1024]{1,0:T(8,128)(2,1)S(1)} %get-tuple-element.90, ...), kind=kLoop, calls=%fused_computation.48 | loop fusion | flops 22020096 | bytes 6291456 | tf_op jit(solution)/shard_map/concatenate | solution.py:76
  476.6 17.1 %collective-permute-done.50 = bf16[704,512]{1,0:T(8,128)(2,1)} collective-permute-done((bf16[704,512]{1,0:T(8,128)(2,1)}, bf16[704,512]{1,0:T(8,128)(2,1)}, u32[]{:S(2)}, u32[]{:S(2)}) %collective-permute-start.50) | collective-permute-done | bytes 720928 | tf_op jit(solution)/shard_map/ppermute | solution.py:56
  507.8 16.6 %convolution_convert_fusion.1 = bf16[1408,2048]{1,0:T(8,128)(2,1)} fusion(bf16[704,1536]{1,0:T(8,128)(2,1)} %get-tuple-element.48, bf16[704,1536]{1,0:T(8,128)(2,1)} %copy-done.96, bf16[768,2048]{1,0:T(8,128)(2,1)} %collective-permute-done.15, bf16[384,1024]{1,0:T(8,128)(2,1)} %copy-done.73, bf16[192,1024]{1,0:T(8,128)(2,1)S(1)} %copy-done.62, ...), kind=kOutput, calls=%fused_computation.24 | convolution fusion | flops 8920236032 | bytes 16384000 | tf_op jit(solution)/shard_map/dot_general | solution.py:15
  542.4 13.2 %fusion = (f32[2,1536]{1,0:T(2,128)S(1)}, f32[1536,1536,2]{1,0,2:T(8,128)}) fusion(f32[1536,1536,2]{1,0,2:T(8,128)} %copy-done.2, f32[2,1536]{1,0:T(2,128)S(1)} %log_add_fusion, pred[1536,1536]{0,1:T(8,128)(4,1)S(1)} %copy-done.3, bf16[1536,2,128]{0,2,1:T(8,128)(2,1)S(1)} %bitcast.232, bf16[1536,128]{0,1:T(8,128)(2,1)S(1)} %copy-done.12, ...), kind=kOutput, calls=%fused_computation.2 | convolution fusion | flops 1227813888 | bytes 41705472 | tf_op jit(solution)/shard_map/qhd,kd->hqk/dot_general | solution.py:236
  555.7 13.7 %fusion.2 = bf16[2,1536,1536]{1,2,0:T(8,128)(2,1)S(1)} fusion(f32[1536,1536,2]{1,0,2:T(8,128)} %get-tuple-element.125, f32[1536,1536,2]{1,0,2:T(8,128)} %copy-done.2, f32[2,1536]{1,0:T(2,128)S(1)} %get-tuple-element.124, f32[2,1536]{1,0:T(2,128)S(1)} %log_add_fusion, pred[1536,1536]{0,1:T(8,128)(4,1)S(1)} %copy-done.3), kind=kLoop, calls=%fused_computation.4 | loop fusion | flops 23592960 | bytes 49569792 | tf_op jit(solution)/shard_map/convert_element_type | solution.py:238
  573.4 12.0 %select_convert_fusion = (bf16[1536,128]{0,1:T(8,128)(2,1)}, f32[1536,128]{0,1:T(8,128)}) fusion(f32[1536,128]{0,1:T(8,128)} %convolution_bitcast_fusion, pred[]{:T(512)S(6)} %eq.48, bf16[1536,2,128]{0,2,1:T(8,128)(2,1)} %bitcast.233, f32[1536,1536,2]{1,0,2:T(8,128)} %copy-done.2, f32[2,1536]{1,0:T(2,128)S(1)} %log_add_fusion, ...), kind=kOutput, calls=%fused_computation.147 | convolution fusion | flops 1222311936 | bytes 23998464 | tf_op jit(solution)/shard_map/hqk,qhd->kd/dot_general | solution.py:241
  600.0 6.7 convolution_convert_fusion.6
  613.4 22.9 %reduce-scatter.9.cloned.1.call-done = bf16[1408,512]{1,0:T(8,128)(2,1)} async-done(((bf16[1408,2048]{1,0:T(8,128)(2,1)}), bf16[1408,512]{1,0:T(8,128)(2,1)}) %reduce-scatter.9.cloned.1.call-update) | async-done | bytes 1441808 | tf_op jit(solution)/shard_map/reduce_scatter | solution.py:225
  650.2 25.0 %reduce-scatter.5.cloned.1.call-done = bf16[384,512]{1,0:T(8,128)(2,1)} async-done(((bf16[384,2048]{1,0:T(8,128)(2,1)}), bf16[384,512]{1,0:T(8,128)(2,1)}) %reduce-scatter.5.cloned.1.call-update) | async-done | bytes 393232 | tf_op jit(solution)/shard_map/reduce_scatter | solution.py:248
  678.5 16.7 %collective-permute-done.44 = bf16[384,512]{1,0:T(8,128)(2,1)S(1)} collective-permute-done((bf16[384,512]{1,0:T(8,128)(2,1)}, bf16[384,512]{1,0:T(8,128)(2,1)S(1)}, u32[]{:S(2)}, u32[]{:S(2)}) %collective-permute-start.44) | collective-permute-done | bytes 393248 | tf_op jit(solution)/shard_map/ppermute | solution.py:56
  718.9 51.3 %psum.7 = f32[2,2048]{1,0:T(2,128)S(1)} all-reduce(f32[2,2048]{1,0:T(2,128)S(1)} %pad_maximum_fusion.26), channel_id=1, replica_groups=mesh['fsdp'=4,'ctx'=4,'tp'=2] {'fsdp','ctx','tp'}, use_global_device_ids=true, to_apply=%region_15.16 | all-reduce | flops 4096 | bytes 32768 | tf_op jit(solution)/shard_map/psum | solution.py:253
  (489 shorter events, 298.6 us)
Async XLA Ops:
  7.2 68.2 %all-gather.5.cloned.1.call-start = ((), (), s32[]{:S(2)}) async-start(), calls=%async_computation.4 | async-start | bytes 2621440 | tf_op jit(solution)/shard_map/all_gather | solution.py:156
  13.6 98.0 %all-gather.7.cloned.1.call-start = ((), (), s32[]{:S(2)}) async-start(), calls=%async_computation.5 | async-start | bytes 1310720 | tf_op jit(solution)/shard_map/all_gather | solution.py:163
  69.3 194.9 %all-gather.9.cloned.1.call-start = ((), (), s32[]{:S(2)}) async-start(), calls=%async_computation.6 | async-start | bytes 7208960 | tf_op jit(solution)/shard_map/all_gather | solution.py:168
  123.4 193.1 %all-gather.11.cloned.1.call-start = ((), (), s32[]{:S(2)}) async-start(), calls=%async_computation.7 | async-start | bytes 3604480 | tf_op jit(solution)/shard_map/all_gather | solution.py:169
  172.8 20.5 %collective-permute-start.23 = (bf16[384,1024]{1,0:T(8,128)(2,1)S(1)}, bf16[384,1024]{1,0:T(8,128)(2,1)S(1)}, u32[]{:S(2)}, u32[]{:S(2)}) collective-permute-start(bf16[384,1024]{1,0:T(8,128)(2,1)S(1)} %pad_maximum_fusion.17), channel_id=1, source_target_pairs={{0,1},{1,0},{2,3},{3,2},{4,5},{5,4},{6,7},{7,6},{8,9},{9,8},{10,11... | collective-permute-start | bytes 2359304 | tf_op jit(solution)/shard_map/ppermute | solution.py:64
  175.0 20.3 %collective-permute-start.25 = (bf16[384,1024]{1,0:T(8,128)(2,1)S(1)}, bf16[384,1024]{1,0:T(8,128)(2,1)S(1)}, u32[]{:S(2)}, u32[]{:S(2)}) collective-permute-start(bf16[384,1024]{1,0:T(8,128)(2,1)S(1)} %pad_maximum_fusion.18), channel_id=1, source_target_pairs={{0,4},{2,6},{4,0},{6,2},{1,5},{3,7},{5,1},{7,3},{8,12},{10,14},{12... | collective-permute-start | bytes 2359304 | tf_op jit(solution)/shard_map/ppermute | solution.py:56
  175.8 39.4 %collective-permute-start.11 = (bf16[192,1024]{1,0:T(8,128)(2,1)S(1)}, bf16[192,1024]{1,0:T(8,128)(2,1)S(1)}, u32[]{:S(2)}, u32[]{:S(2)}) collective-permute-start(bf16[192,1024]{1,0:T(8,128)(2,1)S(1)} %get-tuple-element.99), channel_id=1, source_target_pairs={{0,4},{2,6},{4,0},{6,2},{1,5},{3,7},{5,1},{7,3},{8,12},{10,14},{12... | collective-permute-start | bytes 1179656 | tf_op jit(solution)/shard_map/ppermute | solution.py:56
  177.4 38.6 %collective-permute-start.13 = (bf16[192,1024]{1,0:T(8,128)(2,1)S(1)}, bf16[192,1024]{1,0:T(8,128)(2,1)S(1)}, u32[]{:S(2)}, u32[]{:S(2)}) collective-permute-start(bf16[192,1024]{1,0:T(8,128)(2,1)S(1)} %get-tuple-element.100), channel_id=1, source_target_pairs={{0,1},{1,0},{2,3},{3,2},{4,5},{5,4},{6,7},{7,6},{8,9},{9,8},{10,11... | collective-permute-start | bytes 1179656 | tf_op jit(solution)/shard_map/ppermute | solution.py:64
  215.1 41.8 %collective-permute-start.26 = (bf16[768,2048]{1,0:T(8,128)(2,1)}, bf16[768,2048]{1,0:T(8,128)(2,1)}, u32[]{:S(2)}, u32[]{:S(2)}) collective-permute-start(bf16[768,2048]{1,0:T(8,128)(2,1)} %maximum_maximum_fusion.2), channel_id=1, source_target_pairs={{0,2},{2,0},{4,6},{6,4},{1,3},{3,1},{5,7},{7,5},{8,10},{10,8},{12,... | collective-permute-start | bytes 9437192 | tf_op jit(solution)/shard_map/ppermute | solution.py:60
  215.2 20.0 %collective-permute-start.12 = (bf16[384,1024]{1,0:T(8,128)(2,1)S(1)}, bf16[384,1024]{1,0:T(8,128)(2,1)S(1)}, u32[]{:S(2)}, u32[]{:S(2)}) collective-permute-start(bf16[384,1024]{1,0:T(8,128)(2,1)S(1)} %pad_maximum_fusion.15), channel_id=1, source_target_pairs={{0,1},{1,0},{2,3},{3,2},{4,5},{5,4},{6,7},{7,6},{8,9},{9,8},{10,11... | collective-permute-start | bytes 2359304 | tf_op jit(solution)/shard_map/ppermute | solution.py:64
  256.8 218.0 %reduce-scatter.11.cloned.1.call-start = ((), (), s32[]{:S(2)}) async-start(), calls=%async_computation.11 | async-start | bytes 3604480 | tf_op jit(solution)/shard_map/reduce_scatter | solution.py:226
  363.1 236.0 %reduce-scatter.7.cloned.1.call-start = ((), (), s32[]{:S(2)}) async-start(), calls=%async_computation.9 | async-start | bytes 1310720 | tf_op jit(solution)/shard_map/reduce_scatter | solution.py:232
  367.5 20.5 %collective-permute-start.28 = (bf16[384,1024]{1,0:T(8,128)(2,1)S(1)}, bf16[384,1024]{1,0:T(8,128)(2,1)S(1)}, u32[]{:S(2)}, u32[]{:S(2)}) collective-permute-start(bf16[384,1024]{1,0:T(8,128)(2,1)S(1)} %slice.462), channel_id=1, source_target_pairs={{0,4},{2,6},{4,0},{6,2},{1,5},{3,7},{5,1},{7,3},{8,12},{10,14},{12... | collective-permute-start | bytes 2359304 | tf_op jit(solution)/shard_map/ppermute | solution.py:56
  369.2 20.7 %collective-permute-start.30 = (bf16[384,1024]{1,0:T(8,128)(2,1)S(1)}, bf16[384,1024]{1,0:T(8,128)(2,1)S(1)}, u32[]{:S(2)}, u32[]{:S(2)}) collective-permute-start(bf16[384,1024]{1,0:T(8,128)(2,1)S(1)} %bitcast.230), channel_id=1, source_target_pairs={{0,1},{1,0},{2,3},{3,2},{4,5},{5,4},{6,7},{7,6},{8,9},{9,8},{10,11... | collective-permute-start | bytes 2359304 | tf_op jit(solution)/shard_map/ppermute | solution.py:64
  375.1 29.7 %collective-permute-start.17 = (bf16[384,1024]{1,0:T(8,128)(2,1)S(1)}, bf16[384,1024]{1,0:T(8,128)(2,1)S(1)}, u32[]{:S(2)}, u32[]{:S(2)}) collective-permute-start(bf16[384,1024]{1,0:T(8,128)(2,1)S(1)} %slice.447), channel_id=1, source_target_pairs={{0,4},{2,6},{4,0},{6,2},{1,5},{3,7},{5,1},{7,3},{8,12},{10,14},{12... | collective-permute-start | bytes 2359304 | tf_op jit(solution)/shard_map/ppermute | solution.py:56
  375.9 30.9 %collective-permute-start.19 = (bf16[384,1024]{1,0:T(8,128)(2,1)S(1)}, bf16[384,1024]{1,0:T(8,128)(2,1)S(1)}, u32[]{:S(2)}, u32[]{:S(2)}) collective-permute-start(bf16[384,1024]{1,0:T(8,128)(2,1)S(1)} %bitcast.229), channel_id=1, source_target_pairs={{0,1},{1,0},{2,3},{3,2},{4,5},{5,4},{6,7},{7,6},{8,9},{9,8},{10,11... | collective-permute-start | bytes 2359304 | tf_op jit(solution)/shard_map/ppermute | solution.py:64
  388.4 26.6 %collective-permute-start.29 = (bf16[192,1024]{1,0:T(8,128)(2,1)S(1)}, bf16[192,1024]{1,0:T(8,128)(2,1)S(1)}, u32[]{:S(2)}, u32[]{:S(2)}) collective-permute-start(bf16[192,1024]{1,0:T(8,128)(2,1)S(1)} %slice.464), channel_id=1, source_target_pairs={{0,1},{1,0},{2,3},{3,2},{4,5},{5,4},{6,7},{7,6},{8,9},{9,8},{10,11... | collective-permute-start | bytes 1179656 | tf_op jit(solution)/shard_map/ppermute | solution.py:64
  390.3 25.8 %collective-permute-start.31 = (bf16[192,1024]{1,0:T(8,128)(2,1)S(1)}, bf16[192,1024]{1,0:T(8,128)(2,1)S(1)}, u32[]{:S(2)}, u32[]{:S(2)}) collective-permute-start(bf16[192,1024]{1,0:T(8,128)(2,1)S(1)} %slice.469), channel_id=1, source_target_pairs={{0,4},{2,6},{4,0},{6,2},{1,5},{3,7},{5,1},{7,3},{8,12},{10,14},{12... | collective-permute-start | bytes 1179656 | tf_op jit(solution)/shard_map/ppermute | solution.py:56
  474.8 21.4 %collective-permute-start.36 = (bf16[768,2048]{1,0:T(8,128)(2,1)}, bf16[768,2048]{1,0:T(8,128)(2,1)}, u32[]{:S(2)}, u32[]{:S(2)}) collective-permute-start(bf16[768,2048]{1,0:T(8,128)(2,1)} %maximum_maximum_fusion.3), channel_id=1, source_target_pairs={{0,2},{2,0},{4,6},{6,4},{1,3},{3,1},{5,7},{7,5},{8,10},{10,8},{12,... | collective-permute-start | bytes 9437192 | tf_op jit(solution)/shard_map/ppermute | solution.py:60
  475.5 52.4 %collective-permute-start.21 = (bf16[192,2048]{1,0:T(8,128)(2,1)}, bf16[192,2048]{1,0:T(8,128)(2,1)}, u32[]{:S(2)}, u32[]{:S(2)}) collective-permute-start(bf16[192,2048]{1,0:T(8,128)(2,1)} %get-tuple-element.62), channel_id=1, source_target_pairs={{0,1},{1,0},{2,3},{3,2},{4,5},{5,4},{6,7},{7,6},{8,9},{9,8},{10,11... | collective-permute-start | bytes 2359304 | tf_op jit(solution)/shard_map/ppermute | solution.py:64
  496.2 39.9 %collective-permute-start.51 = (bf16[2,704,512]{2,1,0:T(8,128)(2,1)}, bf16[2,704,512]{2,1,0:T(8,128)(2,1)}, u32[]{:S(2)}, u32[]{:S(2)}) collective-permute-start(bf16[2,704,512]{2,1,0:T(8,128)(2,1)} %pad_maximum_fusion.11), channel_id=1, source_target_pairs={{0,2},{2,0},{4,6},{6,4},{1,3},{3,1},{5,7},{7,5},{8,10},{10,8},{12,... | collective-permute-start | bytes 4325384 | tf_op jit(solution)/shard_map/ppermute | solution.py:60
  507.7 128.7 %reduce-scatter.9.cloned.1.call-start = ((), (), s32[]{:S(2)}) async-start(), calls=%async_computation.10 | async-start | bytes 7208960 | tf_op jit(solution)/shard_map/reduce_scatter | solution.py:225
  524.4 150.8 %reduce-scatter.5.cloned.1.call-start = ((), (), s32[]{:S(2)}) async-start(), calls=%async_computation.8 | async-start | bytes 1966080 | tf_op jit(solution)/shard_map/reduce_scatter | solution.py:248
  599.0 45.2 %collective-permute-start.38 = (bf16[768,2048]{1,0:T(8,128)(2,1)}, bf16[768,2048]{1,0:T(8,128)(2,1)}, u32[]{:S(2)}, u32[]{:S(2)}) collective-permute-start(bf16[768,2048]{1,0:T(8,128)(2,1)} %slice.483), channel_id=1, source_target_pairs={{0,2},{2,0},{4,6},{6,4},{1,3},{3,1},{5,7},{7,5},{8,10},{10,8},{12,... | collective-permute-start | bytes 9437192 | tf_op jit(solution)/shard_map/ppermute | solution.py:60
  608.0 29.8 %collective-permute-start.47 = (bf16[2,256,512]{2,1,0:T(8,128)(2,1)S(1)}, bf16[2,256,512]{2,1,0:T(8,128)(2,1)S(1)}, u32[]{:S(2)}, u32[]{:S(2)}) collective-permute-start(bf16[2,256,512]{2,1,0:T(8,128)(2,1)S(1)} %pad_maximum_fusion.24), channel_id=1, source_target_pairs={{0,2},{2,0},{4,6},{6,4},{1,3},{3,1},{5,7},{7,5},{8,10},{10,8},{12,... | collective-permute-start | bytes 1572872 | tf_op jit(solution)/shard_map/ppermute | solution.py:60
  636.3 59.9 %collective-permute-start.48 = (bf16[1408,512]{1,0:T(8,128)(2,1)}, bf16[1408,512]{1,0:T(8,128)(2,1)}, u32[]{:S(2)}, u32[]{:S(2)}) collective-permute-start(bf16[1408,512]{1,0:T(8,128)(2,1)} %reduce-scatter.9.cloned.1.call-done), channel_id=1, source_target_pairs={{0,4},{2,6},{4,0},{6,2},{1,5},{3,7},{5,1},{7,3},{8,12},{10,14},{12... | collective-permute-start | bytes 4325384 | tf_op jit(solution)/shard_map/ppermute | solution.py:56
  649.8 50.8 %collective-permute-start.39 = (bf16[384,1024]{1,0:T(8,128)(2,1)}, bf16[384,1024]{1,0:T(8,128)(2,1)}, u32[]{:S(2)}, u32[]{:S(2)}) collective-permute-start(bf16[384,1024]{1,0:T(8,128)(2,1)} %slice.485), channel_id=1, source_target_pairs={{0,4},{2,6},{4,0},{6,2},{1,5},{3,7},{5,1},{7,3},{8,12},{10,14},{12... | collective-permute-start | bytes 2359304 | tf_op jit(solution)/shard_map/ppermute | solution.py:56
  675.2 20.0 %collective-permute-start.44 = (bf16[384,512]{1,0:T(8,128)(2,1)}, bf16[384,512]{1,0:T(8,128)(2,1)S(1)}, u32[]{:S(2)}, u32[]{:S(2)}) collective-permute-start(bf16[384,512]{1,0:T(8,128)(2,1)} %reduce-scatter.5.cloned.1.call-done), channel_id=1, source_target_pairs={{0,4},{2,6},{4,0},{6,2},{1,5},{3,7},{5,1},{7,3},{8,12},{10,14},{12... | collective-permute-start | bytes 1179656 | tf_op jit(solution)/shard_map/ppermute | solution.py:56
  676.8 27.1 %collective-permute-start.41 = (bf16[384,1024]{1,0:T(8,128)(2,1)S(1)}, bf16[384,1024]{1,0:T(8,128)(2,1)S(1)}, u32[]{:S(2)}, u32[]{:S(2)}) collective-permute-start(bf16[384,1024]{1,0:T(8,128)(2,1)S(1)} %bitcast.228), channel_id=1, source_target_pairs={{0,1},{1,0},{2,3},{3,2},{4,5},{5,4},{6,7},{7,6},{8,9},{9,8},{10,11... | collective-permute-start | bytes 2359304 | tf_op jit(solution)/shard_map/ppermute | solution.py:64
  696.2 79.2 %collective-permute-start.45 = (bf16[2,384,512]{2,1,0:T(8,128)(2,1)}, bf16[2,384,512]{2,1,0:T(8,128)(2,1)}, u32[]{:S(2)}, u32[]{:S(2)}) collective-permute-start(bf16[2,384,512]{2,1,0:T(8,128)(2,1)} %pad_maximum_fusion.21), channel_id=1, source_target_pairs={{0,2},{2,0},{4,6},{6,4},{1,3},{3,1},{5,7},{7,5},{8,10},{10,8},{12,... | collective-permute-start | bytes 2359304 | tf_op jit(solution)/shard_map/ppermute | solution.py:60
  700.1 87.2 %collective-permute-start.49 = (bf16[2,1408,512]{2,1,0:T(8,128)(2,1)}, bf16[2,1408,512]{2,1,0:T(8,128)(2,1)}, u32[]{:S(2)}, u32[]{:S(2)}) collective-permute-start(bf16[2,1408,512]{2,1,0:T(8,128)(2,1)} %pad_maximum_fusion.5), channel_id=1, source_target_pairs={{0,2},{2,0},{4,6},{6,4},{1,3},{3,1},{5,7},{7,5},{8,10},{10,8},{12,... | collective-permute-start | bytes 8650760 | tf_op jit(solution)/shard_map/ppermute | solution.py:60
  718.1 66.0 %collective-permute-start.43 = (bf16[192,2048]{1,0:T(8,128)(2,1)}, bf16[192,2048]{1,0:T(8,128)(2,1)}, u32[]{:S(2)}, u32[]{:S(2)}) collective-permute-start(bf16[192,2048]{1,0:T(8,128)(2,1)} %fusion.38), channel_id=1, source_target_pairs={{0,1},{1,0},{2,3},{3,2},{4,5},{5,4},{6,7},{7,6},{8,9},{9,8},{10,11... | collective-permute-start | bytes 2359304 | tf_op jit(solution)/shard_map/ppermute | solution.py:64
  (131 other events, 1987.6 us)
Sparse Core Ops, SparseCore 0:
  13.7 48.6 all-gather.4
  69.4 28.4 all-gather.6
  123.5 107.1 all-gather.8
  256.9 59.5 all-gather.10
  363.2 54.9 reduce-scatter.10
  507.8 24.5 reduce-scatter.6
  535.4 100.9 reduce-scatter.8
  639.3 35.8 reduce-scatter.4
where the time goes:
time: 835 us; the launch traced here: 825 us
  waiting for transfers between devices  261 us (31%)
  other arithmetic  209 us (25%)
  matrix products  155 us (19%)
  local copies, waits for them, and re-layouts  83.1 us (10%)
  blocking collectives  51.3 us (6%)
  starting transfers between devices  49.7 us (6%)
  between operations  16.2 us (2%)
    dot_general x12, matrix products, dot(): lax.dot_general(a, b, (((ca,), (cb,)), ((), ())), preferred_element_type=...  111 us
    ppermute x20, waiting for transfers between devices, far(): return lax.ppermute(v, 'ctx', [(i, i ^ 2) for i in range(4)])  105 us
    ppermute x18, waiting for transfers between devices, side(): return lax.ppermute(v, 'tp', [(0, 1), (1, 0)])  88.6 us
    concatenate x4, other arithmetic, spread(): mine = jnp.concatenate([left_all, right_all], axis=1)  79 us
    psum x1, blocking collectives, body(): lax.psum(jnp.stack([jnp.sum(d_n1 * hat_one, axis=0), jnp.sum(d_n2 * hat_t...  51.3 us
    unnamed x208, local copies, waits for them, and re-layouts  27.8 us
    reduce_scatter x1, waiting for transfers between devices, body(): lax.psum_scatter(grad_qkv, 'fsdp', scatter_dimension=1, tiled=True)  25 us
    ppermute x20, starting transfers between devices, far(): return lax.ppermute(v, 'ctx', [(i, i ^ 2) for i in range(4)])  24.6 us
  transfers between devices with their start and end apart: 60, of which 28 were waited for; matrix products, arithmetic and copies ran while one was open for 44% of the time, Pallas kernels for 0%

commit v1 on v0

--- a/solution.py
+++ b/solution.py
@@ -9,6 +9,11 @@
 rope_base = 10000.0
 F32 = jnp.float32
 BF16 = jnp.bfloat16
+
+
+def axis_by_axis(x, one, received):
+    inner = lax.psum(x, one)
+    return lax.psum(inner, received)
 
 
 def dot(a, b, ca, cb):
@@ -250,9 +255,10 @@
     inv_one = lax.rsqrt(jnp.mean(x_own * x_own, axis=-1, keepdims=True) + norm_eps)
     hat_one = x_own * inv_one
     input_grad = both_sides((d_mid + norm_back(d_n1, hat_one, inv_one, gain_one)).astype(BF16), t)
-    gain_grads = lax.psum(
+    gain_grads = axis_by_axis(
         jnp.stack([jnp.sum(d_n1 * hat_one, axis=0), jnp.sum(d_n2 * hat_two, axis=0)]),
-        ("fsdp", "ctx", "tp"),
+        ("ctx", "tp"),
+        "fsdp",
     )
     shard_width = gain_attn.shape[0]
     gain_grads = lax.dynamic_slice_in_dim(

time: 835 us -> 839 us (level)
    psum x1 -> x2, blocking collectives: 51.3 us -> 54.7 us  [the longest x1 36.5 us: axis_by_axis(): inner = lax.psum(x, one)]
where the time goes in v1:
time: 839 us; the launch traced here: 829 us
  waiting for transfers between devices  261 us (31%)
  other arithmetic  209 us (25%)
  matrix products  155 us (18%)
  local copies, waits for them, and re-layouts  83.1 us (10%)
  blocking collectives  54.7 us (7%)
  starting transfers between devices  49.7 us (6%)
  between operations  16.2 us (2%)
    dot_general x12, matrix products, dot(): lax.dot_general(a, b, (((ca,), (cb,)), ((), ())), preferred_element_type=...  111 us
    ppermute x20, waiting for transfers between devices, far(): return lax.ppermute(v, 'ctx', [(i, i ^ 2) for i in range(4)])  105 us
    ppermute x18, waiting for transfers between devices, side(): return lax.ppermute(v, 'tp', [(0, 1), (1, 0)])  88.6 us
    concatenate x4, other arithmetic, spread(): mine = jnp.concatenate([left_all, right_all], axis=1)  79 us
    psum x1, blocking collectives, axis_by_axis(): inner = lax.psum(x, one)  36.5 us
    unnamed x208, local copies, waits for them, and re-layouts  27.9 us
    reduce_scatter x1, waiting for transfers between devices, body(): lax.psum_scatter(grad_qkv, 'fsdp', scatter_dimension=1, tiled=True)  25 us
    ppermute x20, starting transfers between devices, far(): return lax.ppermute(v, 'ctx', [(i, i ^ 2) for i in range(4)])  24.7 us
  transfers between devices with their start and end apart: 60, of which 28 were waited for; matrix products, arithmetic and copies ran while one was open for 44% of the time, Pallas kernels for 0%

profile of v1, /device:TPU:0, one launch (start us, length us, event | category | flops | bytes accessed | tf_op | source)
XLA Modules:
  0.0 828.8 jit_solution(9771869537621604506)
XLA Ops:
  20.2 7.6 collective-permute-done
  31.3 15.3 %collective-permute-done.1 = bf16[384,1024]{1,0:T(8,128)(2,1)S(1)} collective-permute-done((bf16[384,1024]{1,0:T(8,128)(2,1)S(1)}, bf16[384,1024]{1,0:T(8,128)(2,1)S(1)}, u32[]{:S(2)}, u32[]{:S(2)}) %collective-permute-start.1) | collective-permute-done | bytes 786464 | tf_op jit(solution)/shard_map/ppermute | solution.py:69
  47.9 19.6 %maximum_maximum_fusion = bf16[768,2048]{1,0:T(8,128)(2,1)} fusion(bf16[384,1024]{1,0:T(8,128)(2,1)S(1)} %collective-permute-done.3, bf16[192,1024]{1,0:T(8,128)(2,1)S(1)} %collective-permute-done.2, bf16[192,1024]{1,0:T(8,128)(2,1)S(1)} %get-tuple-element.104, bf16[192,1024]{1,0:T(8,128)(2,1)S(1)} %get-tuple-element.102, ...), kind=kLoop, calls=%fused_computation.45 | loop fusion | flops 22020096 | bytes 6291456 | tf_op jit(solution)/shard_map/concatenate | solution.py:81
  103.2 8.3 fusion.16
  132.2 17.4 %collective-permute-done.7 = bf16[384,1024]{1,0:T(8,128)(2,1)S(1)} collective-permute-done((bf16[384,1024]{1,0:T(8,128)(2,1)S(1)}, bf16[384,1024]{1,0:T(8,128)(2,1)S(1)}, u32[]{:S(2)}, u32[]{:S(2)}) %collective-permute-start.7) | collective-permute-done | bytes 786464 | tf_op jit(solution)/shard_map/ppermute | solution.py:61
  152.6 7.9 collective-permute-done.8
  165.9 6.9 collective-permute-done.22
  178.0 15.4 %collective-permute-done.23 = bf16[384,1024]{1,0:T(8,128)(2,1)S(1)} collective-permute-done((bf16[384,1024]{1,0:T(8,128)(2,1)S(1)}, bf16[384,1024]{1,0:T(8,128)(2,1)S(1)}, u32[]{:S(2)}, u32[]{:S(2)}) %collective-permute-start.23) | collective-permute-done | bytes 786464 | tf_op jit(solution)/shard_map/ppermute | solution.py:69
  195.3 19.8 %maximum_maximum_fusion.2 = bf16[768,2048]{1,0:T(8,128)(2,1)} fusion(bf16[384,1024]{1,0:T(8,128)(2,1)S(1)} %collective-permute-done.25, bf16[192,1024]{1,0:T(8,128)(2,1)S(1)} %collective-permute-done.24, bf16[192,1024]{1,0:T(8,128)(2,1)S(1)} %get-tuple-element.96, bf16[192,1024]{1,0:T(8,128)(2,1)S(1)} %get-tuple-element.94, ...), kind=kLoop, calls=%fused_computation.47 | loop fusion | flops 22020096 | bytes 6291456 | tf_op jit(solution)/shard_map/concatenate | solution.py:81
  217.2 18.0 %collective-permute-done.12 = bf16[384,1024]{1,0:T(8,128)(2,1)S(1)} collective-permute-done((bf16[384,1024]{1,0:T(8,128)(2,1)S(1)}, bf16[384,1024]{1,0:T(8,128)(2,1)S(1)}, u32[]{:S(2)}, u32[]{:S(2)}) %collective-permute-start.12) | collective-permute-done | bytes 786464 | tf_op jit(solution)/shard_map/ppermute | solution.py:69
  235.8 20.0 %maximum_maximum_fusion.1 = bf16[768,2048]{1,0:T(8,128)(2,1)} fusion(bf16[384,1024]{1,0:T(8,128)(2,1)S(1)} %collective-permute-done.14, bf16[192,1024]{1,0:T(8,128)(2,1)S(1)} %collective-permute-done.13, bf16[192,1024]{1,0:T(8,128)(2,1)S(1)} %get-tuple-element.100, bf16[192,1024]{1,0:T(8,128)(2,1)S(1)} %get-tuple-element.98, ...), kind=kLoop, calls=%fused_computation.46 | loop fusion | flops 22020096 | bytes 6291456 | tf_op jit(solution)/shard_map/concatenate | solution.py:81
  256.9 7.3 pad_maximum_fusion.2
  264.3 35.0 %fusion.121 = f32[1408,1536]{1,0:T(8,128)} fusion(bf16[1408,2048]{0,1:T(8,128)(2,1)} %all-gather.9.cloned.1.call-done, bf16[768,2048]{1,0:T(8,128)(2,1)} %collective-permute-done.15, bf16[384,1024]{1,0:T(8,128)(2,1)} %copy-done.73, bf16[192,1024]{1,0:T(8,128)(2,1)S(1)} %copy-done.61, bf16[192,1024]{1,0:T(8,128)(2,1)S(1)} %copy-done.42, ...), kind=kOutput, calls=%fused_computation.277 | convolution fusion | flops 8908701696 | bytes 20709376 | tf_op jit(solution)/shard_map/dot_general | solution.py:20
  299.4 17.1 %all-gather.11.cloned.1.call-done = bf16[704,2048]{1,0:T(8,128)(2,1)} async-done(((bf16[704,512]{1,0:T(8,128)(2,1)}), bf16[704,2048]{1,0:T(8,128)(2,1)}) %all-gather.11.cloned.1.call-update) | async-done | bytes 2883600 | tf_op jit(solution)/shard_map/all_gather | solution.py:174
  316.5 13.8 %multiply_convert_fusion.1 = (bf16[704,1536]{1,0:T(8,128)(2,1)S(1)}, bf16[704,1536]{1,0:T(8,128)(2,1)}, bf16[704,1536]{1,0:T(8,128)(2,1)S(1)}) fusion(f32[1408,1536]{1,0:T(8,128)} %fusion.121, bf16[704,2048]{1,0:T(8,128)(2,1)} %all-gather.11.cloned.1.call-done, bf16[1536,2048]{1,0:T(8,128)(2,1)} %pad_maximum_fusion.2), kind=kOutput, calls=%fused_computation.40 | convolution fusion | flops 4445405184 | bytes 24313856 | tf_op jit(solution)/shard_map/dot_general | solution.py:20
  330.3 12.3 %convolution_convert_fusion.3 = bf16[1536,2048]{1,0:T(8,128)(2,1)S(1)} fusion(bf16[1408,2048]{0,1:T(8,128)(2,1)S(1)} %copy-done.93, bf16[704,1536]{1,0:T(8,128)(2,1)} %get-tuple-element.48, bf16[704,1536]{1,0:T(8,128)(2,1)S(1)} %get-tuple-element.47), kind=kOutput, calls=%fused_computation.26 | convolution fusion | flops 8870166528 | bytes 16384000 | tf_op jit(solution)/shard_map/dot_general | solution.py:20
  376.5 11.5 %collective-permute-done.28 = bf16[384,1024]{1,0:T(8,128)(2,1)S(1)} collective-permute-done((bf16[384,1024]{1,0:T(8,128)(2,1)S(1)}, bf16[384,1024]{1,0:T(8,128)(2,1)S(1)}, u32[]{:S(2)}, u32[]{:S(2)}) %collective-permute-start.28) | collective-permute-done | bytes 786464 | tf_op jit(solution)/shard_map/ppermute | solution.py:61
  391.8 13.0 %collective-permute-done.17 = bf16[384,1024]{1,0:T(8,128)(2,1)S(1)} collective-permute-done((bf16[384,1024]{1,0:T(8,128)(2,1)S(1)}, bf16[384,1024]{1,0:T(8,128)(2,1)S(1)}, u32[]{:S(2)}, u32[]{:S(2)}) %collective-permute-start.17) | collective-permute-done | bytes 786464 | tf_op jit(solution)/shard_map/ppermute | solution.py:61
  428.4 7.9 collective-permute-done.32
  438.6 15.2 %collective-permute-done.33 = bf16[384,1024]{1,0:T(8,128)(2,1)S(1)} collective-permute-done((bf16[384,1024]{1,0:T(8,128)(2,1)S(1)}, bf16[384,1024]{1,0:T(8,128)(2,1)S(1)}, u32[]{:S(2)}, u32[]{:S(2)}) %collective-permute-start.33) | collective-permute-done | bytes 786464 | tf_op jit(solution)/shard_map/ppermute | solution.py:69
  455.1 19.7 %maximum_maximum_fusion.3 = bf16[768,2048]{1,0:T(8,128)(2,1)} fusion(bf16[384,1024]{1,0:T(8,128)(2,1)S(1)} %collective-permute-done.35, bf16[192,1024]{1,0:T(8,128)(2,1)S(1)} %collective-permute-done.34, bf16[192,1024]{1,0:T(8,128)(2,1)S(1)} %get-tuple-element.92, bf16[192,1024]{1,0:T(8,128)(2,1)S(1)} %get-tuple-element.90, ...), kind=kLoop, calls=%fused_computation.48 | loop fusion | flops 22020096 | bytes 6291456 | tf_op jit(solution)/shard_map/concatenate | solution.py:81
  476.6 17.1 %collective-permute-done.50 = bf16[704,512]{1,0:T(8,128)(2,1)} collective-permute-done((bf16[704,512]{1,0:T(8,128)(2,1)}, bf16[704,512]{1,0:T(8,128)(2,1)}, u32[]{:S(2)}, u32[]{:S(2)}) %collective-permute-start.50) | collective-permute-done | bytes 720928 | tf_op jit(solution)/shard_map/ppermute | solution.py:61
  507.8 16.6 %convolution_convert_fusion.1 = bf16[1408,2048]{1,0:T(8,128)(2,1)} fusion(bf16[704,1536]{1,0:T(8,128)(2,1)} %get-tuple-element.48, bf16[704,1536]{1,0:T(8,128)(2,1)} %copy-done.96, bf16[768,2048]{1,0:T(8,128)(2,1)} %collective-permute-done.15, bf16[384,1024]{1,0:T(8,128)(2,1)} %copy-done.73, bf16[192,1024]{1,0:T(8,128)(2,1)S(1)} %copy-done.62, ...), kind=kOutput, calls=%fused_computation.24 | convolution fusion | flops 8920236032 | bytes 16384000 | tf_op jit(solution)/shard_map/dot_general | solution.py:20
  542.5 13.2 %fusion = (f32[2,1536]{1,0:T(2,128)S(1)}, f32[1536,1536,2]{1,0,2:T(8,128)}) fusion(f32[1536,1536,2]{1,0,2:T(8,128)} %copy-done.2, f32[2,1536]{1,0:T(2,128)S(1)} %log_add_fusion, pred[1536,1536]{0,1:T(8,128)(4,1)S(1)} %copy-done.3, bf16[1536,2,128]{0,2,1:T(8,128)(2,1)S(1)} %bitcast.232, bf16[1536,128]{0,1:T(8,128)(2,1)S(1)} %copy-done.12, ...), kind=kOutput, calls=%fused_computation.2 | convolution fusion | flops 1227813888 | bytes 41705472 | tf_op jit(solution)/shard_map/qhd,kd->hqk/dot_general | solution.py:241
  555.7 13.7 %fusion.2 = bf16[2,1536,1536]{1,2,0:T(8,128)(2,1)S(1)} fusion(f32[1536,1536,2]{1,0,2:T(8,128)} %get-tuple-element.125, f32[1536,1536,2]{1,0,2:T(8,128)} %copy-done.2, f32[2,1536]{1,0:T(2,128)S(1)} %get-tuple-element.124, f32[2,1536]{1,0:T(2,128)S(1)} %log_add_fusion, pred[1536,1536]{0,1:T(8,128)(4,1)S(1)} %copy-done.3), kind=kLoop, calls=%fused_computation.4 | loop fusion | flops 23592960 | bytes 49569792 | tf_op jit(solution)/shard_map/convert_element_type | solution.py:243
  573.4 12.0 %select_convert_fusion = (bf16[1536,128]{0,1:T(8,128)(2,1)}, f32[1536,128]{0,1:T(8,128)}) fusion(f32[1536,128]{0,1:T(8,128)} %convolution_bitcast_fusion, pred[]{:T(512)S(6)} %eq.48, bf16[1536,2,128]{0,2,1:T(8,128)(2,1)} %bitcast.233, f32[1536,1536,2]{1,0,2:T(8,128)} %copy-done.2, f32[2,1536]{1,0:T(2,128)S(1)} %log_add_fusion, ...), kind=kOutput, calls=%fused_computation.147 | convolution fusion | flops 1222311936 | bytes 23998464 | tf_op jit(solution)/shard_map/hqk,qhd->kd/dot_general | solution.py:246
  600.0 6.7 convolution_convert_fusion.6
  613.4 22.9 %reduce-scatter.9.cloned.1.call-done = bf16[1408,512]{1,0:T(8,128)(2,1)} async-done(((bf16[1408,2048]{1,0:T(8,128)(2,1)}), bf16[1408,512]{1,0:T(8,128)(2,1)}) %reduce-scatter.9.cloned.1.call-update) | async-done | bytes 1441808 | tf_op jit(solution)/shard_map/reduce_scatter | solution.py:230
  650.2 25.0 %reduce-scatter.5.cloned.1.call-done = bf16[384,512]{1,0:T(8,128)(2,1)} async-done(((bf16[384,2048]{1,0:T(8,128)(2,1)}), bf16[384,512]{1,0:T(8,128)(2,1)}) %reduce-scatter.5.cloned.1.call-update) | async-done | bytes 393232 | tf_op jit(solution)/shard_map/reduce_scatter | solution.py:253
  678.5 16.7 %collective-permute-done.44 = bf16[384,512]{1,0:T(8,128)(2,1)S(1)} collective-permute-done((bf16[384,512]{1,0:T(8,128)(2,1)}, bf16[384,512]{1,0:T(8,128)(2,1)S(1)}, u32[]{:S(2)}, u32[]{:S(2)}) %collective-permute-start.44) | collective-permute-done | bytes 393248 | tf_op jit(solution)/shard_map/ppermute | solution.py:61
  718.9 36.5 %psum.14 = f32[2,2048]{1,0:T(2,128)S(1)} all-reduce(f32[2,2048]{1,0:T(2,128)S(1)} %pad_maximum_fusion.26), channel_id=1, replica_groups=mesh['fsdp'=4,'ctx'=4,'tp'=2] {'ctx','tp'}, use_global_device_ids=true, to_apply=%region_15.16 | all-reduce | flops 4096 | bytes 32768 | tf_op jit(solution)/shard_map/psum | solution.py:15
  755.4 18.2 %psum.15 = f32[2,2048]{1,0:T(2,128)S(1)} all-reduce(f32[2,2048]{1,0:T(2,128)S(1)} %psum.14), channel_id=1, replica_groups=mesh['fsdp'=4,'ctx'=4,'tp'=2] {'fsdp'}, use_global_device_ids=true, to_apply=%region_16.17 | all-reduce | flops 4096 | bytes 32768 | tf_op jit(solution)/shard_map/psum | solution.py:16
  (490 shorter events, 305.0 us)
Async XLA Ops:
  7.2 68.2 %all-gather.5.cloned.1.call-start = ((), (), s32[]{:S(2)}) async-start(), calls=%async_computation.4 | async-start | bytes 2621440 | tf_op jit(solution)/shard_map/all_gather | solution.py:161
  13.6 97.9 %all-gather.7.cloned.1.call-start = ((), (), s32[]{:S(2)}) async-start(), calls=%async_computation.5 | async-start | bytes 1310720 | tf_op jit(solution)/shard_map/all_gather | solution.py:168
  69.3 195.0 %all-gather.9.cloned.1.call-start = ((), (), s32[]{:S(2)}) async-start(), calls=%async_computation.6 | async-start | bytes 7208960 | tf_op jit(solution)/shard_map/all_gather | solution.py:173
  123.4 193.2 %all-gather.11.cloned.1.call-start = ((), (), s32[]{:S(2)}) async-start(), calls=%async_computation.7 | async-start | bytes 3604480 | tf_op jit(solution)/shard_map/all_gather | solution.py:174
  172.8 20.5 %collective-permute-start.23 = (bf16[384,1024]{1,0:T(8,128)(2,1)S(1)}, bf16[384,1024]{1,0:T(8,128)(2,1)S(1)}, u32[]{:S(2)}, u32[]{:S(2)}) collective-permute-start(bf16[384,1024]{1,0:T(8,128)(2,1)S(1)} %pad_maximum_fusion.17), channel_id=1, source_target_pairs={{0,1},{1,0},{2,3},{3,2},{4,5},{5,4},{6,7},{7,6},{8,9},{9,8},{10,11... | collective-permute-start | bytes 2359304 | tf_op jit(solution)/shard_map/ppermute | solution.py:69
  175.0 20.3 %collective-permute-start.25 = (bf16[384,1024]{1,0:T(8,128)(2,1)S(1)}, bf16[384,1024]{1,0:T(8,128)(2,1)S(1)}, u32[]{:S(2)}, u32[]{:S(2)}) collective-permute-start(bf16[384,1024]{1,0:T(8,128)(2,1)S(1)} %pad_maximum_fusion.18), channel_id=1, source_target_pairs={{0,4},{2,6},{4,0},{6,2},{1,5},{3,7},{5,1},{7,3},{8,12},{10,14},{12... | collective-permute-start | bytes 2359304 | tf_op jit(solution)/shard_map/ppermute | solution.py:61
  175.8 39.4 %collective-permute-start.11 = (bf16[192,1024]{1,0:T(8,128)(2,1)S(1)}, bf16[192,1024]{1,0:T(8,128)(2,1)S(1)}, u32[]{:S(2)}, u32[]{:S(2)}) collective-permute-start(bf16[192,1024]{1,0:T(8,128)(2,1)S(1)} %get-tuple-element.99), channel_id=1, source_target_pairs={{0,4},{2,6},{4,0},{6,2},{1,5},{3,7},{5,1},{7,3},{8,12},{10,14},{12... | collective-permute-start | bytes 1179656 | tf_op jit(solution)/shard_map/ppermute | solution.py:61
  177.5 38.5 %collective-permute-start.13 = (bf16[192,1024]{1,0:T(8,128)(2,1)S(1)}, bf16[192,1024]{1,0:T(8,128)(2,1)S(1)}, u32[]{:S(2)}, u32[]{:S(2)}) collective-permute-start(bf16[192,1024]{1,0:T(8,128)(2,1)S(1)} %get-tuple-element.100), channel_id=1, source_target_pairs={{0,1},{1,0},{2,3},{3,2},{4,5},{5,4},{6,7},{7,6},{8,9},{9,8},{10,11... | collective-permute-start | bytes 1179656 | tf_op jit(solution)/shard_map/ppermute | solution.py:69
  215.1 41.8 %collective-permute-start.26 = (bf16[768,2048]{1,0:T(8,128)(2,1)}, bf16[768,2048]{1,0:T(8,128)(2,1)}, u32[]{:S(2)}, u32[]{:S(2)}) collective-permute-start(bf16[768,2048]{1,0:T(8,128)(2,1)} %maximum_maximum_fusion.2), channel_id=1, source_target_pairs={{0,2},{2,0},{4,6},{6,4},{1,3},{3,1},{5,7},{7,5},{8,10},{10,8},{12,... | collective-permute-start | bytes 9437192 | tf_op jit(solution)/shard_map/ppermute | solution.py:65
  215.2 20.0 %collective-permute-start.12 = (bf16[384,1024]{1,0:T(8,128)(2,1)S(1)}, bf16[384,1024]{1,0:T(8,128)(2,1)S(1)}, u32[]{:S(2)}, u32[]{:S(2)}) collective-permute-start(bf16[384,1024]{1,0:T(8,128)(2,1)S(1)} %pad_maximum_fusion.15), channel_id=1, source_target_pairs={{0,1},{1,0},{2,3},{3,2},{4,5},{5,4},{6,7},{7,6},{8,9},{9,8},{10,11... | collective-permute-start | bytes 2359304 | tf_op jit(solution)/shard_map/ppermute | solution.py:69
  256.9 218.0 %reduce-scatter.11.cloned.1.call-start = ((), (), s32[]{:S(2)}) async-start(), calls=%async_computation.11 | async-start | bytes 3604480 | tf_op jit(solution)/shard_map/reduce_scatter | solution.py:231
  363.1 235.9 %reduce-scatter.7.cloned.1.call-start = ((), (), s32[]{:S(2)}) async-start(), calls=%async_computation.9 | async-start | bytes 1310720 | tf_op jit(solution)/shard_map/reduce_scatter | solution.py:237
  367.6 20.5 %collective-permute-start.28 = (bf16[384,1024]{1,0:T(8,128)(2,1)S(1)}, bf16[384,1024]{1,0:T(8,128)(2,1)S(1)}, u32[]{:S(2)}, u32[]{:S(2)}) collective-permute-start(bf16[384,1024]{1,0:T(8,128)(2,1)S(1)} %slice.462), channel_id=1, source_target_pairs={{0,4},{2,6},{4,0},{6,2},{1,5},{3,7},{5,1},{7,3},{8,12},{10,14},{12... | collective-permute-start | bytes 2359304 | tf_op jit(solution)/shard_map/ppermute | solution.py:61
  369.2 20.7 %collective-permute-start.30 = (bf16[384,1024]{1,0:T(8,128)(2,1)S(1)}, bf16[384,1024]{1,0:T(8,128)(2,1)S(1)}, u32[]{:S(2)}, u32[]{:S(2)}) collective-permute-start(bf16[384,1024]{1,0:T(8,128)(2,1)S(1)} %bitcast.230), channel_id=1, source_target_pairs={{0,1},{1,0},{2,3},{3,2},{4,5},{5,4},{6,7},{7,6},{8,9},{9,8},{10,11... | collective-permute-start | bytes 2359304 | tf_op jit(solution)/shard_map/ppermute | solution.py:69
  375.1 29.7 %collective-permute-start.17 = (bf16[384,1024]{1,0:T(8,128)(2,1)S(1)}, bf16[384,1024]{1,0:T(8,128)(2,1)S(1)}, u32[]{:S(2)}, u32[]{:S(2)}) collective-permute-start(bf16[384,1024]{1,0:T(8,128)(2,1)S(1)} %slice.447), channel_id=1, source_target_pairs={{0,4},{2,6},{4,0},{6,2},{1,5},{3,7},{5,1},{7,3},{8,12},{10,14},{12... | collective-permute-start | bytes 2359304 | tf_op jit(solution)/shard_map/ppermute | solution.py:61
  375.9 30.9 %collective-permute-start.19 = (bf16[384,1024]{1,0:T(8,128)(2,1)S(1)}, bf16[384,1024]{1,0:T(8,128)(2,1)S(1)}, u32[]{:S(2)}, u32[]{:S(2)}) collective-permute-start(bf16[384,1024]{1,0:T(8,128)(2,1)S(1)} %bitcast.229), channel_id=1, source_target_pairs={{0,1},{1,0},{2,3},{3,2},{4,5},{5,4},{6,7},{7,6},{8,9},{9,8},{10,11... | collective-permute-start | bytes 2359304 | tf_op jit(solution)/shard_map/ppermute | solution.py:69
  388.4 26.6 %collective-permute-start.29 = (bf16[192,1024]{1,0:T(8,128)(2,1)S(1)}, bf16[192,1024]{1,0:T(8,128)(2,1)S(1)}, u32[]{:S(2)}, u32[]{:S(2)}) collective-permute-start(bf16[192,1024]{1,0:T(8,128)(2,1)S(1)} %slice.464), channel_id=1, source_target_pairs={{0,1},{1,0},{2,3},{3,2},{4,5},{5,4},{6,7},{7,6},{8,9},{9,8},{10,11... | collective-permute-start | bytes 1179656 | tf_op jit(solution)/shard_map/ppermute | solution.py:69
  390.3 25.8 %collective-permute-start.31 = (bf16[192,1024]{1,0:T(8,128)(2,1)S(1)}, bf16[192,1024]{1,0:T(8,128)(2,1)S(1)}, u32[]{:S(2)}, u32[]{:S(2)}) collective-permute-start(bf16[192,1024]{1,0:T(8,128)(2,1)S(1)} %slice.469), channel_id=1, source_target_pairs={{0,4},{2,6},{4,0},{6,2},{1,5},{3,7},{5,1},{7,3},{8,12},{10,14},{12... | collective-permute-start | bytes 1179656 | tf_op jit(solution)/shard_map/ppermute | solution.py:61
  474.8 21.4 %collective-permute-start.36 = (bf16[768,2048]{1,0:T(8,128)(2,1)}, bf16[768,2048]{1,0:T(8,128)(2,1)}, u32[]{:S(2)}, u32[]{:S(2)}) collective-permute-start(bf16[768,2048]{1,0:T(8,128)(2,1)} %maximum_maximum_fusion.3), channel_id=1, source_target_pairs={{0,2},{2,0},{4,6},{6,4},{1,3},{3,1},{5,7},{7,5},{8,10},{10,8},{12,... | collective-permute-start | bytes 9437192 | tf_op jit(solution)/shard_map/ppermute | solution.py:65
  475.5 52.3 %collective-permute-start.21 = (bf16[192,2048]{1,0:T(8,128)(2,1)}, bf16[192,2048]{1,0:T(8,128)(2,1)}, u32[]{:S(2)}, u32[]{:S(2)}) collective-permute-start(bf16[192,2048]{1,0:T(8,128)(2,1)} %get-tuple-element.62), channel_id=1, source_target_pairs={{0,1},{1,0},{2,3},{3,2},{4,5},{5,4},{6,7},{7,6},{8,9},{9,8},{10,11... | collective-permute-start | bytes 2359304 | tf_op jit(solution)/shard_map/ppermute | solution.py:69
  496.2 39.9 %collective-permute-start.51 = (bf16[2,704,512]{2,1,0:T(8,128)(2,1)}, bf16[2,704,512]{2,1,0:T(8,128)(2,1)}, u32[]{:S(2)}, u32[]{:S(2)}) collective-permute-start(bf16[2,704,512]{2,1,0:T(8,128)(2,1)} %pad_maximum_fusion.11), channel_id=1, source_target_pairs={{0,2},{2,0},{4,6},{6,4},{1,3},{3,1},{5,7},{7,5},{8,10},{10,8},{12,... | collective-permute-start | bytes 4325384 | tf_op jit(solution)/shard_map/ppermute | solution.py:65
  507.7 128.7 %reduce-scatter.9.cloned.1.call-start = ((), (), s32[]{:S(2)}) async-start(), calls=%async_computation.10 | async-start | bytes 7208960 | tf_op jit(solution)/shard_map/reduce_scatter | solution.py:230
  524.4 150.8 %reduce-scatter.5.cloned.1.call-start = ((), (), s32[]{:S(2)}) async-start(), calls=%async_computation.8 | async-start | bytes 1966080 | tf_op jit(solution)/shard_map/reduce_scatter | solution.py:253
  599.0 45.1 %collective-permute-start.38 = (bf16[768,2048]{1,0:T(8,128)(2,1)}, bf16[768,2048]{1,0:T(8,128)(2,1)}, u32[]{:S(2)}, u32[]{:S(2)}) collective-permute-start(bf16[768,2048]{1,0:T(8,128)(2,1)} %slice.483), channel_id=1, source_target_pairs={{0,2},{2,0},{4,6},{6,4},{1,3},{3,1},{5,7},{7,5},{8,10},{10,8},{12,... | collective-permute-start | bytes 9437192 | tf_op jit(solution)/shard_map/ppermute | solution.py:65
  608.0 29.8 %collective-permute-start.47 = (bf16[2,256,512]{2,1,0:T(8,128)(2,1)S(1)}, bf16[2,256,512]{2,1,0:T(8,128)(2,1)S(1)}, u32[]{:S(2)}, u32[]{:S(2)}) collective-permute-start(bf16[2,256,512]{2,1,0:T(8,128)(2,1)S(1)} %pad_maximum_fusion.24), channel_id=1, source_target_pairs={{0,2},{2,0},{4,6},{6,4},{1,3},{3,1},{5,7},{7,5},{8,10},{10,8},{12,... | collective-permute-start | bytes 1572872 | tf_op jit(solution)/shard_map/ppermute | solution.py:65
  636.4 60.0 %collective-permute-start.48 = (bf16[1408,512]{1,0:T(8,128)(2,1)}, bf16[1408,512]{1,0:T(8,128)(2,1)}, u32[]{:S(2)}, u32[]{:S(2)}) collective-permute-start(bf16[1408,512]{1,0:T(8,128)(2,1)} %reduce-scatter.9.cloned.1.call-done), channel_id=1, source_target_pairs={{0,4},{2,6},{4,0},{6,2},{1,5},{3,7},{5,1},{7,3},{8,12},{10,14},{12... | collective-permute-start | bytes 4325384 | tf_op jit(solution)/shard_map/ppermute | solution.py:61
  649.8 50.9 %collective-permute-start.39 = (bf16[384,1024]{1,0:T(8,128)(2,1)}, bf16[384,1024]{1,0:T(8,128)(2,1)}, u32[]{:S(2)}, u32[]{:S(2)}) collective-permute-start(bf16[384,1024]{1,0:T(8,128)(2,1)} %slice.485), channel_id=1, source_target_pairs={{0,4},{2,6},{4,0},{6,2},{1,5},{3,7},{5,1},{7,3},{8,12},{10,14},{12... | collective-permute-start | bytes 2359304 | tf_op jit(solution)/shard_map/ppermute | solution.py:61
  675.2 20.1 %collective-permute-start.44 = (bf16[384,512]{1,0:T(8,128)(2,1)}, bf16[384,512]{1,0:T(8,128)(2,1)S(1)}, u32[]{:S(2)}, u32[]{:S(2)}) collective-permute-start(bf16[384,512]{1,0:T(8,128)(2,1)} %reduce-scatter.5.cloned.1.call-done), channel_id=1, source_target_pairs={{0,4},{2,6},{4,0},{6,2},{1,5},{3,7},{5,1},{7,3},{8,12},{10,14},{12... | collective-permute-start | bytes 1179656 | tf_op jit(solution)/shard_map/ppermute | solution.py:61
  676.8 27.1 %collective-permute-start.41 = (bf16[384,1024]{1,0:T(8,128)(2,1)S(1)}, bf16[384,1024]{1,0:T(8,128)(2,1)S(1)}, u32[]{:S(2)}, u32[]{:S(2)}) collective-permute-start(bf16[384,1024]{1,0:T(8,128)(2,1)S(1)} %bitcast.228), channel_id=1, source_target_pairs={{0,1},{1,0},{2,3},{3,2},{4,5},{5,4},{6,7},{7,6},{8,9},{9,8},{10,11... | collective-permute-start | bytes 2359304 | tf_op jit(solution)/shard_map/ppermute | solution.py:69
  696.3 82.4 %collective-permute-start.45 = (bf16[2,384,512]{2,1,0:T(8,128)(2,1)}, bf16[2,384,512]{2,1,0:T(8,128)(2,1)}, u32[]{:S(2)}, u32[]{:S(2)}) collective-permute-start(bf16[2,384,512]{2,1,0:T(8,128)(2,1)} %pad_maximum_fusion.21), channel_id=1, source_target_pairs={{0,2},{2,0},{4,6},{6,4},{1,3},{3,1},{5,7},{7,5},{8,10},{10,8},{12,... | collective-permute-start | bytes 2359304 | tf_op jit(solution)/shard_map/ppermute | solution.py:65
  700.2 90.5 %collective-permute-start.49 = (bf16[2,1408,512]{2,1,0:T(8,128)(2,1)}, bf16[2,1408,512]{2,1,0:T(8,128)(2,1)}, u32[]{:S(2)}, u32[]{:S(2)}) collective-permute-start(bf16[2,1408,512]{2,1,0:T(8,128)(2,1)} %pad_maximum_fusion.5), channel_id=1, source_target_pairs={{0,2},{2,0},{4,6},{6,4},{1,3},{3,1},{5,7},{7,5},{8,10},{10,8},{12,... | collective-permute-start | bytes 8650760 | tf_op jit(solution)/shard_map/ppermute | solution.py:65
  718.1 69.3 %collective-permute-start.43 = (bf16[192,2048]{1,0:T(8,128)(2,1)}, bf16[192,2048]{1,0:T(8,128)(2,1)}, u32[]{:S(2)}, u32[]{:S(2)}) collective-permute-start(bf16[192,2048]{1,0:T(8,128)(2,1)} %fusion.38), channel_id=1, source_target_pairs={{0,1},{1,0},{2,3},{3,2},{4,5},{5,4},{6,7},{7,6},{8,9},{9,8},{10,11... | collective-permute-start | bytes 2359304 | tf_op jit(solution)/shard_map/ppermute | solution.py:69
  (131 other events, 1994.3 us)
Sparse Core Ops, SparseCore 0:
  13.7 48.6 all-gather.4
  69.4 28.4 all-gather.6
  123.5 107.1 all-gather.8
  256.9 59.5 all-gather.10
  363.2 54.9 reduce-scatter.10
  507.8 24.6 reduce-scatter.6
  535.4 100.9 reduce-scatter.8
  639.4 35.7 reduce-scatter.4
